TPU v7x, 32 devices: a whole 2x2x4 slice. The times are simulated.
32 devices in a mesh: mode: 4 (over y, x), space: 8 (over z, core).
Axes of the slice: x: 2, y: 2, z: 4, core: 2. Of those that a mesh axis runs over, the one named last changes fastest.
Arguments:
- resident: bfloat16 [2, 4096, 8, 2048], P(None, 'mode', None, 'space'), may hold values from -0.09375 to 0.09375
- source: bfloat16 [2, 384, 8, 2048], P(None, 'mode', None, 'space'), may hold values from -6 to 6
- insertion: bfloat16 [4, 384, 1024], replicated, may hold values from -0.3125 to 0.3125
- owners: int32 [128, 1], P('mode'), may hold values from 0 to 7; in each aligned block of 32 rows (0 to 31, 32 to 63, ...) at most 4 rows name the same one
- diag_time: int32 [4], replicated, may hold values from 0 to 7
- diag_mom: int32 [4], replicated, may hold values from 1 to 4
Outputs:
- mesons: bfloat16 [32, 2, 512, 1024], P('space', None, 'mode')
Inputs may be any that keep to these rules, and one draw needn't show every extreme that they name: `owners`: within the 32 strips of one index of mode, no owner is named more than 4 times.
All inputs are finite; a program needn't handle non-finite values.
Results may differ from a plain program's by a relative error of at most 0.019.
Values may be sent and summed in bfloat16 or wider, within the bound.
A program may use at most 192 MiB of HBM per device.

v0:
```python
import functools
import math

import jax
import jax.numpy as jnp
from jax import lax
from jax.experimental import pallas as pl
from jax.experimental.pallas import tpu as pltpu
from jax.sharding import PartitionSpec as P

STRIP = 128
LX = 96
CAP = 4
AHEAD = 3
PICK = 32
DEPTH = 3
MESH = pl.DeviceIdType.MESH


def phase_pair(diag_mom, start, count):
    lattice_positions = (start + jnp.arange(count, dtype=jnp.int32)) % LX
    turns = diag_mom[:, None] * lattice_positions[None, :] % LX
    angle = 2.0 * math.pi / LX * turns.astype(jnp.float32)
    return (jnp.cos(angle), jnp.sin(angle))


def pick_rows(rows, times, time):
    row = lax.broadcasted_iota(jnp.int32, (rows, rows * times), 0)
    col = lax.broadcasted_iota(jnp.int32, (rows, rows * times), 1)
    return jnp.where(col == row * times + time, 1.0, 0.0).astype(jnp.bfloat16)


def field_kernel(
    n_mode, n_space, blocks, times, time_ref, strip_ref, cos_ref, sin_ref, res_hbm, src_hbm, ins_hbm, out_hbm, *scratch
):
    others = scratch[:n_mode - 1]
    (a_ref, s_ref, pick, res_buf, src_buf, out_ref, ins, mine, theirs, came, acc, field,
     src_sem, res_sem, out_sem, ins_sem, gs_sem, gr_sem, ps_sem, pr_sem, zs_sem, zr_sem) = scratch[n_mode - 1:]
    diagrams = s_ref.shape[0]
    chunk = STRIP * times
    sources = (s_ref,) + others
    src_dev = s_ref.shape[1] // 2
    n_line = n_space // 2
    steps = n_line * CAP
    me = lax.axis_index("space")
    mode = lax.axis_index("mode")
    z, core = me // 2, me % 2
    partner = z * 2 + 1 - core

    barrier = pltpu.get_barrier_semaphore()

    def greet(space, other_mode):
        pl.semaphore_signal(barrier, inc=1, device_id=(other_mode, space), device_id_type=MESH)

    def fetch(b):
        rows = pl.ds(pl.multiple_of(b * chunk, chunk), chunk)
        return pltpu.make_async_copy(res_hbm.at[:, rows, :], res_buf.at[b % DEPTH], res_sem.at[b % DEPTH])

    src_copy = pltpu.make_async_copy(src_hbm, src_buf, src_sem)
    ins_copy = pltpu.make_async_copy(ins_hbm, ins, ins_sem)
    src_copy.start()
    for b in range(DEPTH):
        fetch(b).start()
    greet(partner, mode)

    @pl.when(z > 0)
    def _():
        greet(me - 2, mode)

    @pl.when(z < n_line - 1)
    def _():
        greet(me + 2, mode)

    for q in range(1, n_mode):
        greet(me, (mode + q) % n_mode)

    taken = PICK * times
    for d in range(diagrams):
        pick[d * PICK:(d + 1) * PICK, :] = pick_rows(PICK, times, time_ref[d])
    src_copy.wait()
    for part in range(src_dev // PICK):
        for p in range(2):
            chosen = jnp.dot(
                pick[...], src_buf[p, part * taken:(part + 1) * taken, :],
                preferred_element_type=jnp.float32,
            ).astype(jnp.bfloat16)
            first = p * src_dev + part * PICK
            for d in range(diagrams):
                s_ref[d, first:first + PICK, :] = chosen[d * PICK:(d + 1) * PICK]
    pl.semaphore_wait(barrier, n_mode + jnp.minimum(z, 1) + jnp.minimum(n_line - 1 - z, 1))

    def gather(q):
        return pltpu.make_async_remote_copy(
            src_ref=s_ref, dst_ref=others[q - 1], send_sem=gs_sem.at[q - 1], recv_sem=gr_sem.at[q - 1],
            device_id=((mode + n_mode - q) % n_mode, me), device_id_type=MESH,
        )

    for q in range(1, n_mode):
        gather(q).start()

    def phase(b, carry):
        fetch(b).wait()
        for part in range(STRIP // PICK):
            span = slice(part * taken, (part + 1) * taken)
            real = jnp.dot(pick[...], res_buf[b % DEPTH, 0, span, :], preferred_element_type=jnp.float32)
            imag = jnp.dot(pick[...], res_buf[b % DEPTH, 1, span, :], preferred_element_type=jnp.float32)
            for d in range(diagrams):
                own = slice(d * PICK, (d + 1) * PICK)
                cosine, sine = cos_ref[d:d + 1, :], sin_ref[d:d + 1, :]
                first = part * PICK
                a_ref[d * blocks + b, first:first + PICK, :] = (
                    real[own] * cosine - imag[own] * sine
                ).astype(jnp.bfloat16)
                a_ref[d * blocks + b, STRIP + first:STRIP + first + PICK, :] = (
                    -(real[own] * sine + imag[own] * cosine)
                ).astype(jnp.bfloat16)

        @pl.when(b + DEPTH < blocks)
        def _():
            fetch(b + DEPTH).start()

        return carry

    lax.fori_loop(0, blocks, phase, 0)
    ins_copy.start()

    def place(k):
        s, j = k // CAP, k % CAP
        low = z < n_line // 2
        near = jnp.where(low, z, n_line - 1 - z)
        turn = s // 2
        t = jnp.where(s < 2 * near, turn + (1 - s % 2) * (n_line - 1 - 2 * turn), n_line - 1 - (s - near))
        return jnp.where(low, t, n_line - 1 - t) * CAP + j

    def term(slot, source):
        strip = strip_ref[slot]
        both = lax.dot_general(
            source[strip // blocks], a_ref[strip], (((1,), (1,)), ((), ())),
            preferred_element_type=jnp.float32,
        )
        real = both[:src_dev, :STRIP] - both[src_dev:, STRIP:]
        imag = both[src_dev:, :STRIP] + both[:src_dev, STRIP:]
        return real, imag

    def across(line_slot, q):
        return pltpu.make_async_remote_copy(
            src_ref=theirs.at[line_slot, q], dst_ref=mine.at[line_slot, q],
            send_sem=ps_sem.at[line_slot, q], recv_sem=pr_sem.at[line_slot, q],
            device_id=(mode, partner), device_id_type=MESH,
        )

    def along(line_slot, landing, q, step):
        return pltpu.make_async_remote_copy(
            src_ref=mine.at[line_slot, q], dst_ref=came.at[landing, q],
            send_sem=zs_sem.at[line_slot, q], recv_sem=zr_sem.at[landing, q],
            device_id=(mode, me + step), device_id_type=MESH,
        )

    def slot_of(line_slot, its_core):
        return (line_slot // CAP * 2 + its_core) * CAP + line_slot % CAP

    def give(line_slot, q):
        real, imag = term(slot_of(line_slot, 1 - core), sources[q])
        theirs[line_slot, q, :src_dev, :] = real.astype(jnp.bfloat16)
        theirs[line_slot, q, src_dev:, :] = imag.astype(jnp.bfloat16)
        across(line_slot, q).start()

    def sum_of_chip(line_slot, q):
        real, imag = term(slot_of(line_slot, core), sources[q])
        across(line_slot, q).wait_recv()
        acc[:src_dev, :] = real + mine[line_slot, q, :src_dev, :].astype(jnp.float32)
        acc[src_dev:, :] = imag + mine[line_slot, q, src_dev:, :].astype(jnp.float32)

    def add_arrival(landing, q):
        along(0, landing, q, 0).wait_recv()
        acc[...] += came[landing, q].astype(jnp.float32)

    def run(count, order, body, q):
        def first(k, carry):
            give(order(k), q)
            return carry

        def step(k, carry):
            @pl.when(k + AHEAD < count)
            def _():
                give(order(k + AHEAD), q)

            body(order(k), q)
            return carry

        lax.fori_loop(0, min(AHEAD, count), first, 0)
        lax.fori_loop(0, count, step, 0)

    def transit(line_slot, q):
        t = line_slot // CAP
        sum_of_chip(line_slot, q)

        @pl.when((t > z) & (z > 0))
        def _():
            add_arrival(line_slot + CAP, q)

        @pl.when((t < z) & (z < n_line - 1))
        def _():
            add_arrival(line_slot, q)

        mine[line_slot, q] = acc[...].astype(jnp.bfloat16)

        @pl.when(t > z)
        def _():
            along(line_slot, line_slot + CAP, q, 2).start()

        @pl.when(t < z)
        def _():
            along(line_slot, line_slot, q, -2).start()

    def give_out(j):
        return pltpu.make_async_copy(out_ref.at[j], out_hbm.at[j], out_sem.at[j])

    def arrive(line_slot, q):
        j = line_slot % CAP
        sum_of_chip(line_slot, q)

        @pl.when(z > 0)
        def _():
            add_arrival(line_slot + CAP, q)

        @pl.when(z < n_line - 1)
        def _():
            add_arrival(line_slot, q)

        rows = pl.ds(pl.multiple_of((mode + q) % n_mode * src_dev, 16), src_dev)
        field[j, rows, :STRIP] = acc[:src_dev, :].astype(jnp.bfloat16)
        field[j, rows, STRIP:] = acc[src_dev:, :].astype(jnp.bfloat16)
        if q == n_mode - 1:
            product = lax.dot_general(
                field[j], ins[strip_ref[slot_of(line_slot, core)] // blocks], (((0,), (0,)), ((), ())),
                preferred_element_type=jnp.float32,
            )
            out_ref[j] = product.astype(jnp.bfloat16)
            give_out(j).start()

    for q in range(n_mode + 1):
        if 0 < q < n_mode:
            gather(q).wait_recv()
        if q < n_mode:
            run(steps - CAP, place, transit, q)
        if q == n_mode:
            ins_copy.wait()
        if q > 0:
            run(CAP, lambda k: z * CAP + k, arrive, q - 1)

    for j in range(CAP):
        give_out(j).wait()
    for q in range(1, n_mode):
        gather(q).wait_send()

    def drain(line_slot, carry):
        for q in range(n_mode):
            across(line_slot, q).wait_send()

            @pl.when(line_slot // CAP != z)
            def _(q=q):
                along(line_slot, line_slot, q, 0).wait_send()
        return carry

    lax.fori_loop(0, steps, drain, 0)


def on_device(resident, source, insertion, owners, diag_time, diag_mom):
    _, res_dev, times, slab = resident.shape
    src_dev = source.shape[1]
    n_mode = lax.axis_size("mode")
    n_space = lax.axis_size("space")
    diagrams, src, width = insertion.shape
    blocks = res_dev // STRIP
    strip_count = diagrams * blocks
    slots = n_space * CAP
    me_space = lax.axis_index("space")
    cosine, sine = phase_pair(diag_mom, me_space * slab, slab)

    owner_list = owners[:, 0]
    order = jnp.arange(strip_count, dtype=jnp.int32)
    same = owner_list[:, None] == owner_list[None, :]
    rank = jnp.sum((same & (order[None, :] < order[:, None])).astype(jnp.int32), axis=1)
    slot = owner_list * CAP + rank
    slot_numbers = jnp.arange(slots, dtype=jnp.int32)
    match = slot[None, :] == slot_numbers[:, None]
    slot_strip = jnp.sum(jnp.where(match, order[None, :], 0), axis=1)

    bf16 = jnp.bfloat16
    steps = n_space // 2 * CAP
    piece = (n_mode, 2 * src_dev, STRIP)
    dma = pltpu.SemaphoreType.DMA
    vmem = pl.BlockSpec(memory_space=pltpu.VMEM)
    hbm = pl.BlockSpec(memory_space=pltpu.HBM)
    smem = pl.BlockSpec(memory_space=pltpu.SMEM)
    buffers = [pltpu.VMEM((diagrams, 2 * src_dev, slab), bf16)] * (n_mode - 1) + [
        pltpu.VMEM((strip_count, 2 * STRIP, slab), bf16),
        pltpu.VMEM((diagrams, 2 * src_dev, slab), bf16),
        pltpu.VMEM((diagrams * PICK, PICK * times), bf16),
        pltpu.VMEM((DEPTH, 2, STRIP * times, slab), bf16),
        pltpu.VMEM((2, src_dev * times, slab), bf16),
        pltpu.VMEM((CAP, 2 * STRIP, width), bf16),
        pltpu.VMEM((diagrams, src, width), bf16),
        pltpu.VMEM((steps,) + piece, bf16),
        pltpu.VMEM((steps,) + piece, bf16),
        pltpu.VMEM((steps + CAP,) + piece, bf16),
        pltpu.VMEM((2 * src_dev, STRIP), jnp.float32),
        pltpu.VMEM((CAP, src, 2 * STRIP), bf16),
    ]
    semaphores = [
        dma(()),
        dma((DEPTH,)),
        dma((CAP,)),
        dma(()),
        dma((n_mode - 1,)),
        dma((n_mode - 1,)),
        dma((steps, n_mode)),
        dma((steps, n_mode)),
        dma((steps, n_mode)),
        dma((steps + CAP, n_mode)),
    ]
    mesons = pl.pallas_call(
        functools.partial(field_kernel, n_mode, n_space, blocks, times),
        in_specs=[smem, smem, vmem, vmem, hbm, hbm, hbm],
        out_specs=pl.BlockSpec(memory_space=pl.ANY),
        out_shape=jax.ShapeDtypeStruct((CAP, 2 * STRIP, width), bf16),
        scratch_shapes=buffers + semaphores,
        compiler_params=pltpu.CompilerParams(
            collective_id=0, has_side_effects=True, vmem_limit_bytes=67043328
        ),
        name="field",
    )(
        diag_time, slot_strip, cosine, sine, resident.reshape(2, res_dev * times, slab),
        source.reshape(2, src_dev * times, slab), insertion,
    )
    mesons = mesons.reshape(CAP, 2, STRIP, width)
    if strip_count < slots:
        filled = lax.dynamic_slice_in_dim(jnp.any(match, axis=1), me_space * CAP, CAP)
        mesons = jnp.where(filled[:, None, None, None], mesons, jnp.zeros_like(mesons))
    return mesons


def solution(mesh):
    in_specs = (
        P(None, "mode", None, "space"),
        P(None, "mode", None, "space"),
        P(),
        P("mode", None),
        P(),
        P(),
    )
    out_specs = P("space", None, "mode", None)
    return jax.shard_map(
        on_device, mesh=mesh, in_specs=in_specs, out_specs=out_specs, check_vma=False
    )
```

profile of v0, /device:TPU:9, one launch (start us, length us, event | category | flops | bytes accessed | tf_op | source)
XLA Modules:
  0.0 75.3 jit_solution(7916558740783040000)
XLA Ops:
  0.0 0.9 %convert_reduce_fusion = s32[32]{0:T(128)S(1)} fusion(s32[32]{0:T(128)} %bitcast.8), kind=kLoop, calls=%fused_computation.2 | loop fusion | flops 5088 | bytes 256 | tf_op jit(solution)/shard_map/reduce_sum | solution.py:284
  0.9 0.7 multiply_add_fusion
  1.6 0.7 select_reduce_fusion.strip_ref
  2.2 1.4 %fusion.6 = (f32[4,256]{1,0:T(4,128)}, f32[4,256]{1,0:T(4,128)}) fusion(s32[256]{0:T(256)S(1)} %and_select_fusion, s32[4]{0:T(128)} %param.11), kind=kLoop, calls=%fused_computation.12 | loop fusion | flops 9216 | bytes 9232 | tf_op jit(solution)/shard_map/sin | solution.py:24
  3.6 68.6 %field.1 = bf16[4,256,1024]{2,1,0:T(8,128)(2,1)} custom-call(s32[4]{0:T(128)} %time_ref.1, s32[32]{0:T(128)} %select_reduce_fusion.strip_ref, f32[4,256]{1,0:T(4,128)} %get-tuple-element.6.cos_ref, f32[4,256]{1,0:T(4,128)} %get-tuple-element.5.sin_ref, bf16[2,8192,256]{2,1,0:T(8,128)(2,1)} %bitcast.6, bf16[2,768,256]{2,1,0:T(8,128)(2,1)} %bitcast.7, ...), custom_call_target="tpu_custom_call" | custom-call | tf_op jit(solution)/shard_map/field/pallas_call | solution.py:323
  72.2 3.1 %copy.8 = bf16[4,2,128,1024]{3,2,1,0:T(8,128)(2,1)} copy(bf16[4,2,128,1024]{3,2,1,0:T(8,128)(2,1)} %bitcast.5) | data formatting | bytes 4194304
  (1 shorter events, 0.0 us)
where the time goes:
time: 75.5 us; the launch traced here: 75.3 us
  Pallas kernels  68.6 us (91%)
  other arithmetic  3.63 us (5%)
  local copies, waits for them, and re-layouts  3.08 us (4%)
    pallas_call x1, Pallas kernels, on_device(): pl.pallas_call(functools.partial(field_kernel, n_mode, n_space, blocks, t...  68.6 us
    unnamed x1, local copies, waits for them, and re-layouts  3.08 us

commit v1 on v0

--- a/solution.py
+++ b/solution.py
@@ -13,15 +13,41 @@
 CAP = 4
 AHEAD = 3
 PICK = 32
-DEPTH = 3
+VMEM = 67043328
+SPARE = 1 << 20
 MESH = pl.DeviceIdType.MESH
 
 
-def phase_pair(diag_mom, start, count):
-    lattice_positions = (start + jnp.arange(count, dtype=jnp.int32)) % LX
-    turns = diag_mom[:, None] * lattice_positions[None, :] % LX
-    angle = 2.0 * math.pi / LX * turns.astype(jnp.float32)
+def wrapped(count):
+    return count - LX * jnp.floor((count + 0.5) * (1.0 / LX))
+
+
+def phase_pair(mom_ref, start, diagrams, count):
+    row = lax.broadcasted_iota(jnp.int32, (diagrams, count), 0)
+    site = lax.broadcasted_iota(jnp.int32, (diagrams, count), 1) + start % LX
+    momentum = jnp.zeros((diagrams, count), jnp.int32)
+    for d in range(diagrams):
+        momentum = jnp.where(row == d, mom_ref[d], momentum)
+    turns = wrapped(momentum.astype(jnp.float32) * wrapped(site.astype(jnp.float32)))
+    angle = 2.0 * math.pi / LX * turns
     return (jnp.cos(angle), jnp.sin(angle))
+
+
+def fill_slots(owner_ref, strip_ref, n_space):
+    count = owner_ref.shape[0]
+    bits = (count - 1).bit_length()
+
+    def of_owner(o, carry):
+        packed, unit = jnp.int32(0), jnp.int32(1)
+        for k in range(count):
+            named = owner_ref[k] == o
+            packed = jnp.where(named, packed + k * unit, packed)
+            unit = jnp.where(named, unit * (1 << bits), unit)
+        for c in range(CAP):
+            strip_ref[o * CAP + c] = packed // (1 << bits * c) % (1 << bits)
+        return carry
+
+    lax.fori_loop(0, n_space, of_owner, 0)
 
 
 def pick_rows(rows, times, time):
@@ -31,11 +57,12 @@
 
 
 def field_kernel(
-    n_mode, n_space, blocks, times, time_ref, strip_ref, cos_ref, sin_ref, res_hbm, src_hbm, ins_hbm, out_hbm, *scratch
+    n_mode, n_space, blocks, times, depth, time_hbm, mom_hbm, owner_hbm, res_hbm, src_hbm, ins_hbm, out_ref, *scratch
 ):
     others = scratch[:n_mode - 1]
-    (a_ref, s_ref, pick, res_buf, src_buf, out_ref, ins, mine, theirs, came, acc, field,
-     src_sem, res_sem, out_sem, ins_sem, gs_sem, gr_sem, ps_sem, pr_sem, zs_sem, zr_sem) = scratch[n_mode - 1:]
+    (a_ref, s_ref, pick, res_buf, src_buf, ins, mine, theirs, came, acc, field, cos_ref, sin_ref,
+     time_ref, mom_ref, owner_ref, strip_ref,
+     small_sem, src_sem, res_sem, ins_sem, gs_sem, gr_sem, ps_sem, pr_sem, zs_sem, zr_sem) = scratch[n_mode - 1:]
     diagrams = s_ref.shape[0]
     chunk = STRIP * times
     sources = (s_ref,) + others
@@ -52,14 +79,30 @@
     def greet(space, other_mode):
         pl.semaphore_signal(barrier, inc=1, device_id=(other_mode, space), device_id_type=MESH)
 
+    def other_mode(q, sign):
+        if n_mode & (n_mode - 1):
+            return (mode + n_mode + sign * q) % n_mode
+        there, bit = 0, 1
+        while bit < n_mode:
+            ours = mode // bit % 2
+            there += bit * (1 - ours if q & bit else ours)
+            bit *= 2
+        return there
+
     def fetch(b):
         rows = pl.ds(pl.multiple_of(b * chunk, chunk), chunk)
-        return pltpu.make_async_copy(res_hbm.at[:, rows, :], res_buf.at[b % DEPTH], res_sem.at[b % DEPTH])
+        return pltpu.make_async_copy(res_hbm.at[:, rows, :], res_buf.at[b % depth], res_sem.at[b % depth])
 
     src_copy = pltpu.make_async_copy(src_hbm, src_buf, src_sem)
     ins_copy = pltpu.make_async_copy(ins_hbm, ins, ins_sem)
+    small = [
+        pltpu.make_async_copy(there, here, small_sem.at[i])
+        for i, (there, here) in enumerate(((time_hbm, time_ref), (mom_hbm, mom_ref), (owner_hbm, owner_ref)))
+    ]
+    for copy in small:
+        copy.start()
     src_copy.start()
-    for b in range(DEPTH):
+    for b in range(depth):
         fetch(b).start()
     greet(partner, mode)
 
@@ -72,11 +115,15 @@
         greet(me + 2, mode)
 
     for q in range(1, n_mode):
-        greet(me, (mode + q) % n_mode)
+        greet(me, other_mode(q, 1))
 
     taken = PICK * times
+    for copy in small:
+        copy.wait()
     for d in range(diagrams):
         pick[d * PICK:(d + 1) * PICK, :] = pick_rows(PICK, times, time_ref[d])
+    fill_slots(owner_ref, strip_ref, n_space)
+    cos_ref[...], sin_ref[...] = phase_pair(mom_ref, me * cos_ref.shape[1], diagrams, cos_ref.shape[1])
     src_copy.wait()
     for part in range(src_dev // PICK):
         for p in range(2):
@@ -92,7 +139,7 @@
     def gather(q):
         return pltpu.make_async_remote_copy(
             src_ref=s_ref, dst_ref=others[q - 1], send_sem=gs_sem.at[q - 1], recv_sem=gr_sem.at[q - 1],
-            device_id=((mode + n_mode - q) % n_mode, me), device_id_type=MESH,
+            device_id=(other_mode(q, -1), me), device_id_type=MESH,
         )
 
     for q in range(1, n_mode):
@@ -102,8 +149,8 @@
         fetch(b).wait()
         for part in range(STRIP // PICK):
             span = slice(part * taken, (part + 1) * taken)
-            real = jnp.dot(pick[...], res_buf[b % DEPTH, 0, span, :], preferred_element_type=jnp.float32)
-            imag = jnp.dot(pick[...], res_buf[b % DEPTH, 1, span, :], preferred_element_type=jnp.float32)
+            real = jnp.dot(pick[...], res_buf[b % depth, 0, span, :], preferred_element_type=jnp.float32)
+            imag = jnp.dot(pick[...], res_buf[b % depth, 1, span, :], preferred_element_type=jnp.float32)
             for d in range(diagrams):
                 own = slice(d * PICK, (d + 1) * PICK)
                 cosine, sine = cos_ref[d:d + 1, :], sin_ref[d:d + 1, :]
@@ -115,9 +162,9 @@
                     -(real[own] * sine + imag[own] * cosine)
                 ).astype(jnp.bfloat16)
 
-        @pl.when(b + DEPTH < blocks)
-        def _():
-            fetch(b + DEPTH).start()
+        @pl.when(b + depth < blocks)
+        def _():
+            fetch(b + depth).start()
 
         return carry
 
@@ -213,9 +260,6 @@
         def _():
             along(line_slot, line_slot, q, -2).start()
 
-    def give_out(j):
-        return pltpu.make_async_copy(out_ref.at[j], out_hbm.at[j], out_sem.at[j])
-
     def arrive(line_slot, q):
         j = line_slot % CAP
         sum_of_chip(line_slot, q)
@@ -228,7 +272,7 @@
         def _():
             add_arrival(line_slot, q)
 
-        rows = pl.ds(pl.multiple_of((mode + q) % n_mode * src_dev, 16), src_dev)
+        rows = pl.ds(pl.multiple_of(other_mode(q, 1) * src_dev, 16), src_dev)
         field[j, rows, :STRIP] = acc[:src_dev, :].astype(jnp.bfloat16)
         field[j, rows, STRIP:] = acc[src_dev:, :].astype(jnp.bfloat16)
         if q == n_mode - 1:
@@ -237,7 +281,6 @@
                 preferred_element_type=jnp.float32,
             )
             out_ref[j] = product.astype(jnp.bfloat16)
-            give_out(j).start()
 
     for q in range(n_mode + 1):
         if 0 < q < n_mode:
@@ -249,8 +292,6 @@
         if q > 0:
             run(CAP, lambda k: z * CAP + k, arrive, q - 1)
 
-    for j in range(CAP):
-        give_out(j).wait()
     for q in range(1, n_mode):
         gather(q).wait_send()
 
@@ -276,16 +317,7 @@
     strip_count = diagrams * blocks
     slots = n_space * CAP
     me_space = lax.axis_index("space")
-    cosine, sine = phase_pair(diag_mom, me_space * slab, slab)
-
     owner_list = owners[:, 0]
-    order = jnp.arange(strip_count, dtype=jnp.int32)
-    same = owner_list[:, None] == owner_list[None, :]
-    rank = jnp.sum((same & (order[None, :] < order[:, None])).astype(jnp.int32), axis=1)
-    slot = owner_list * CAP + rank
-    slot_numbers = jnp.arange(slots, dtype=jnp.int32)
-    match = slot[None, :] == slot_numbers[:, None]
-    slot_strip = jnp.sum(jnp.where(match, order[None, :], 0), axis=1)
 
     bf16 = jnp.bfloat16
     steps = n_space // 2 * CAP
@@ -293,25 +325,34 @@
     dma = pltpu.SemaphoreType.DMA
     vmem = pl.BlockSpec(memory_space=pltpu.VMEM)
     hbm = pl.BlockSpec(memory_space=pltpu.HBM)
-    smem = pl.BlockSpec(memory_space=pltpu.SMEM)
     buffers = [pltpu.VMEM((diagrams, 2 * src_dev, slab), bf16)] * (n_mode - 1) + [
         pltpu.VMEM((strip_count, 2 * STRIP, slab), bf16),
         pltpu.VMEM((diagrams, 2 * src_dev, slab), bf16),
         pltpu.VMEM((diagrams * PICK, PICK * times), bf16),
-        pltpu.VMEM((DEPTH, 2, STRIP * times, slab), bf16),
+        None,
         pltpu.VMEM((2, src_dev * times, slab), bf16),
-        pltpu.VMEM((CAP, 2 * STRIP, width), bf16),
         pltpu.VMEM((diagrams, src, width), bf16),
         pltpu.VMEM((steps,) + piece, bf16),
         pltpu.VMEM((steps,) + piece, bf16),
         pltpu.VMEM((steps + CAP,) + piece, bf16),
         pltpu.VMEM((2 * src_dev, STRIP), jnp.float32),
         pltpu.VMEM((CAP, src, 2 * STRIP), bf16),
+        pltpu.VMEM((diagrams, slab), jnp.float32),
+        pltpu.VMEM((diagrams, slab), jnp.float32),
+        pltpu.SMEM((diagrams,), jnp.int32),
+        pltpu.SMEM((diagrams,), jnp.int32),
+        pltpu.SMEM((strip_count,), jnp.int32),
+        pltpu.SMEM((slots,), jnp.int32),
     ]
+    block = pltpu.VMEM((1, 2, STRIP * times, slab), bf16)
+    held = [math.prod(b.shape) * b.dtype.itemsize for b in buffers + [block] if b is not None]
+    limit = VMEM - CAP * 2 * STRIP * width * 2 - SPARE // 4
+    depth = max(2, min(blocks, (limit - SPARE - sum(held[:-1])) // held[-1]))
+    buffers[n_mode + 2] = pltpu.VMEM((depth, 2, STRIP * times, slab), bf16)
     semaphores = [
+        dma((3,)),
         dma(()),
-        dma((DEPTH,)),
-        dma((CAP,)),
+        dma((depth,)),
         dma(()),
         dma((n_mode - 1,)),
         dma((n_mode - 1,)),
@@ -321,22 +362,23 @@
         dma((steps + CAP, n_mode)),
     ]
     mesons = pl.pallas_call(
-        functools.partial(field_kernel, n_mode, n_space, blocks, times),
-        in_specs=[smem, smem, vmem, vmem, hbm, hbm, hbm],
-        out_specs=pl.BlockSpec(memory_space=pl.ANY),
-        out_shape=jax.ShapeDtypeStruct((CAP, 2 * STRIP, width), bf16),
+        functools.partial(field_kernel, n_mode, n_space, blocks, times, depth),
+        in_specs=[hbm] * 6,
+        out_specs=vmem,
+        out_shape=pltpu.VMEM((CAP, 2 * STRIP, width), bf16),
         scratch_shapes=buffers + semaphores,
         compiler_params=pltpu.CompilerParams(
-            collective_id=0, has_side_effects=True, vmem_limit_bytes=67043328
+            collective_id=0, has_side_effects=True, vmem_limit_bytes=limit
         ),
         name="field",
     )(
-        diag_time, slot_strip, cosine, sine, resident.reshape(2, res_dev * times, slab),
+        diag_time, diag_mom, owner_list, resident.reshape(2, res_dev * times, slab),
         source.reshape(2, src_dev * times, slab), insertion,
     )
     mesons = mesons.reshape(CAP, 2, STRIP, width)
     if strip_count < slots:
-        filled = lax.dynamic_slice_in_dim(jnp.any(match, axis=1), me_space * CAP, CAP)
+        taken = jnp.sum((owner_list == me_space).astype(jnp.int32))
+        filled = jnp.arange(CAP, dtype=jnp.int32) < taken
         mesons = jnp.where(filled[:, None, None, None], mesons, jnp.zeros_like(mesons))
     return mesons
 

time: 75.5 us -> 68.6 us (0.909)
  other arithmetic: 3.63 us -> 0 us
  local copies, waits for them, and re-layouts: 3.08 us -> 1.32 us
  Pallas kernels: 68.6 us -> 67.1 us
    unnamed x1, local copies, waits for them, and re-layouts: 3.08 us -> 1.32 us
    reduce_sum x2 -> x0, other arithmetic: 1.57 us -> none  [the longest x1 0.91 us: on_device(): jnp.sum((same & (order[None, :] < order[:, None])).astype(jnp.int32), axi...]
    pallas_call x1, Pallas kernels: 68.6 us -> 67.1 us  [on_device(): pl.pallas_call(functools.partial(field_kernel, n_mode, n_space, blocks, t...]
    sin x1 -> x0, other arithmetic: 1.38 us -> none  [phase_pair(): return (jnp.cos(angle), jnp.sin(angle))]
where the time goes in v1:
time: 68.6 us; the launch traced here: 68.5 us
  Pallas kernels  67.1 us (98%)
  local copies, waits for them, and re-layouts  1.32 us (2%)
    pallas_call x1, Pallas kernels, on_device(): pl.pallas_call(functools.partial(field_kernel, n_mode, n_space, blocks, t...  67.1 us

profile of v1, /device:TPU:9, one launch (start us, length us, event | category | flops | bytes accessed | tf_op | source)
XLA Modules:
  0.0 68.5 jit_solution(216178307281177298)
XLA Ops:
  0.0 67.1 %field.1 = bf16[4,256,1024]{2,1,0:T(8,128)(2,1)S(1)} custom-call(s32[4]{0:T(128)} %time_hbm.1, s32[4]{0:T(128)} %mom_hbm.1, s32[32]{0:T(128)} %bitcast.7, bf16[2,8192,256]{2,1,0:T(8,128)(2,1)} %bitcast.5, bf16[2,768,256]{2,1,0:T(8,128)(2,1)} %bitcast.6, bf16[4,384,1024]{2,1,0:T(8,128)(2,1)} %ins_hbm.1), custom_call_target="tpu_custom_call" | custom-call | tf_op jit(solution)/shard_map/field/pallas_call | solution.py:364
  67.2 1.3 %copy.8 = bf16[4,2,128,1024]{3,2,1,0:T(8,128)(2,1)} copy(bf16[4,2,128,1024]{3,2,1,0:T(8,128)(2,1)S(1)} %bitcast.4) | data formatting | bytes 4194304

commit v2 on v1

--- a/solution.py
+++ b/solution.py
@@ -11,7 +11,9 @@
 STRIP = 128
 LX = 96
 CAP = 4
-AHEAD = 3
+AHEAD = 4
+RING = 2 * AHEAD + 2
+WAVES = (2, 2, 1, 1)
 PICK = 32
 VMEM = 67043328
 SPARE = 1 << 20
@@ -102,8 +104,13 @@
     for copy in small:
         copy.start()
     src_copy.start()
-    for b in range(depth):
-        fetch(b).start()
+    flight = min(sum(WAVES), depth)
+
+    def wave(n):
+        for b in range(sum(WAVES[:n]), min(sum(WAVES[:n + 1]), flight)):
+            fetch(b).start()
+
+    wave(0)
     greet(partner, mode)
 
     @pl.when(z > 0)
@@ -120,11 +127,13 @@
     taken = PICK * times
     for copy in small:
         copy.wait()
+    wave(1)
     for d in range(diagrams):
         pick[d * PICK:(d + 1) * PICK, :] = pick_rows(PICK, times, time_ref[d])
     fill_slots(owner_ref, strip_ref, n_space)
     cos_ref[...], sin_ref[...] = phase_pair(mom_ref, me * cos_ref.shape[1], diagrams, cos_ref.shape[1])
     src_copy.wait()
+    wave(2)
     for part in range(src_dev // PICK):
         for p in range(2):
             chosen = jnp.dot(
@@ -134,16 +143,7 @@
             first = p * src_dev + part * PICK
             for d in range(diagrams):
                 s_ref[d, first:first + PICK, :] = chosen[d * PICK:(d + 1) * PICK]
-    pl.semaphore_wait(barrier, n_mode + jnp.minimum(z, 1) + jnp.minimum(n_line - 1 - z, 1))
-
-    def gather(q):
-        return pltpu.make_async_remote_copy(
-            src_ref=s_ref, dst_ref=others[q - 1], send_sem=gs_sem.at[q - 1], recv_sem=gr_sem.at[q - 1],
-            device_id=(other_mode(q, -1), me), device_id_type=MESH,
-        )
-
-    for q in range(1, n_mode):
-        gather(q).start()
+    wave(3)
 
     def phase(b, carry):
         fetch(b).wait()
@@ -162,13 +162,24 @@
                     -(real[own] * sine + imag[own] * cosine)
                 ).astype(jnp.bfloat16)
 
-        @pl.when(b + depth < blocks)
-        def _():
-            fetch(b + depth).start()
+        @pl.when(b + flight < blocks)
+        def _():
+            fetch(b + flight).start()
 
         return carry
 
     lax.fori_loop(0, blocks, phase, 0)
+    pl.semaphore_wait(barrier, n_mode + jnp.minimum(z, 1) + jnp.minimum(n_line - 1 - z, 1))
+
+    def gather(q):
+        return pltpu.make_async_remote_copy(
+            src_ref=s_ref, dst_ref=others[q - 1], send_sem=gs_sem.at[q - 1], recv_sem=gr_sem.at[q - 1],
+            device_id=(other_mode(q, -1), me), device_id_type=MESH,
+        )
+
+    for q in range(1, n_mode):
+        gather(q).start()
+
     ins_copy.start()
 
     def place(k):
@@ -189,58 +200,75 @@
         imag = both[src_dev:, :STRIP] + both[:src_dev, STRIP:]
         return real, imag
 
-    def across(line_slot, q):
+    def across(line_slot, q, turn):
         return pltpu.make_async_remote_copy(
             src_ref=theirs.at[line_slot, q], dst_ref=mine.at[line_slot, q],
-            send_sem=ps_sem.at[line_slot, q], recv_sem=pr_sem.at[line_slot, q],
+            send_sem=ps_sem, recv_sem=pr_sem.at[turn % RING],
             device_id=(mode, partner), device_id_type=MESH,
         )
 
+    def arrival(landing, q):
+        if q < n_mode - 1:
+            return q * (n_line + 1) + landing // CAP
+        return q * (n_line + 1) + landing
+
+    def group(landing):
+        near = pl.ds(0, CAP)
+        return pltpu.make_async_remote_copy(
+            src_ref=came.at[0, near], dst_ref=came.at[0, near], send_sem=zs_sem, recv_sem=zr_sem.at[landing],
+            device_id=(mode, partner), device_id_type=MESH,
+        )
+
     def along(line_slot, landing, q, step):
         return pltpu.make_async_remote_copy(
-            src_ref=mine.at[line_slot, q], dst_ref=came.at[landing, q],
-            send_sem=zs_sem.at[line_slot, q], recv_sem=zr_sem.at[landing, q],
+            src_ref=mine.at[line_slot, q], dst_ref=came.at[q, landing],
+            send_sem=zs_sem, recv_sem=zr_sem.at[arrival(landing, q)],
             device_id=(mode, me + step), device_id_type=MESH,
         )
 
     def slot_of(line_slot, its_core):
         return (line_slot // CAP * 2 + its_core) * CAP + line_slot % CAP
 
-    def give(line_slot, q):
+    def give(line_slot, q, turn):
         real, imag = term(slot_of(line_slot, 1 - core), sources[q])
         theirs[line_slot, q, :src_dev, :] = real.astype(jnp.bfloat16)
         theirs[line_slot, q, src_dev:, :] = imag.astype(jnp.bfloat16)
-        across(line_slot, q).start()
-
-    def sum_of_chip(line_slot, q):
+        across(line_slot, q, turn).start()
+
+    def sum_of_chip(line_slot, q, turn):
         real, imag = term(slot_of(line_slot, core), sources[q])
-        across(line_slot, q).wait_recv()
+        across(line_slot, q, turn).wait_recv()
         acc[:src_dev, :] = real + mine[line_slot, q, :src_dev, :].astype(jnp.float32)
         acc[src_dev:, :] = imag + mine[line_slot, q, src_dev:, :].astype(jnp.float32)
 
     def add_arrival(landing, q):
-        along(0, landing, q, 0).wait_recv()
-        acc[...] += came[landing, q].astype(jnp.float32)
-
-    def run(count, order, body, q):
+        if q < n_mode - 1:
+            @pl.when(landing % CAP == 0)
+            def _():
+                group(arrival(landing, q)).wait_recv()
+        else:
+            along(0, landing, q, 0).wait_recv()
+        acc[...] += came[q, landing].astype(jnp.float32)
+
+    def run(count, order, body, q, turn):
         def first(k, carry):
-            give(order(k), q)
+            give(order(k), q, turn + k)
             return carry
 
         def step(k, carry):
             @pl.when(k + AHEAD < count)
             def _():
-                give(order(k + AHEAD), q)
-
-            body(order(k), q)
+                give(order(k + AHEAD), q, turn + k + AHEAD)
+
+            body(order(k), q, turn + k)
             return carry
 
         lax.fori_loop(0, min(AHEAD, count), first, 0)
         lax.fori_loop(0, count, step, 0)
 
-    def transit(line_slot, q):
+    def transit(line_slot, q, turn):
         t = line_slot // CAP
-        sum_of_chip(line_slot, q)
+        sum_of_chip(line_slot, q, turn)
 
         @pl.when((t > z) & (z > 0))
         def _():
@@ -260,9 +288,9 @@
         def _():
             along(line_slot, line_slot, q, -2).start()
 
-    def arrive(line_slot, q):
+    def arrive(line_slot, q, turn):
         j = line_slot % CAP
-        sum_of_chip(line_slot, q)
+        sum_of_chip(line_slot, q, turn)
 
         @pl.when(z > 0)
         def _():
@@ -282,29 +310,32 @@
             )
             out_ref[j] = product.astype(jnp.bfloat16)
 
+    turn = 0
     for q in range(n_mode + 1):
         if 0 < q < n_mode:
             gather(q).wait_recv()
         if q < n_mode:
-            run(steps - CAP, place, transit, q)
+            run(steps - CAP, place, transit, q, turn)
+            turn += steps - CAP
         if q == n_mode:
             ins_copy.wait()
         if q > 0:
-            run(CAP, lambda k: z * CAP + k, arrive, q - 1)
+            run(CAP, lambda k: z * CAP + k, arrive, q - 1, turn)
+            turn += CAP
 
     for q in range(1, n_mode):
         gather(q).wait_send()
-
-    def drain(line_slot, carry):
-        for q in range(n_mode):
-            across(line_slot, q).wait_send()
-
-            @pl.when(line_slot // CAP != z)
-            def _(q=q):
-                along(line_slot, line_slot, q, 0).wait_send()
-        return carry
-
-    lax.fori_loop(0, steps, drain, 0)
+    everything = pltpu.make_async_remote_copy(
+        src_ref=theirs, dst_ref=mine, send_sem=ps_sem, recv_sem=pr_sem.at[0],
+        device_id=(mode, partner), device_id_type=MESH,
+    )
+    everything.wait_send()
+    sent = pl.ds(0, steps - CAP)
+    passed_on = pltpu.make_async_remote_copy(
+        src_ref=theirs.at[sent], dst_ref=mine.at[sent], send_sem=zs_sem, recv_sem=pr_sem.at[0],
+        device_id=(mode, partner), device_id_type=MESH,
+    )
+    passed_on.wait_send()
 
 
 def on_device(resident, source, insertion, owners, diag_time, diag_mom):
@@ -334,7 +365,7 @@
         pltpu.VMEM((diagrams, src, width), bf16),
         pltpu.VMEM((steps,) + piece, bf16),
         pltpu.VMEM((steps,) + piece, bf16),
-        pltpu.VMEM((steps + CAP,) + piece, bf16),
+        pltpu.VMEM((n_mode, steps + CAP) + piece[1:], bf16),
         pltpu.VMEM((2 * src_dev, STRIP), jnp.float32),
         pltpu.VMEM((CAP, src, 2 * STRIP), bf16),
         pltpu.VMEM((diagrams, slab), jnp.float32),
@@ -356,10 +387,10 @@
         dma(()),
         dma((n_mode - 1,)),
         dma((n_mode - 1,)),
-        dma((steps, n_mode)),
-        dma((steps, n_mode)),
-        dma((steps, n_mode)),
-        dma((steps + CAP, n_mode)),
+        dma(()),
+        dma((RING,)),
+        dma(()),
+        dma(((n_mode - 1) * (n_space // 2 + 1) + steps + CAP,)),
     ]
     mesons = pl.pallas_call(
         functools.partial(field_kernel, n_mode, n_space, blocks, times, depth),

time: 68.6 us -> 66.5 us (0.969)
  Pallas kernels: 67.1 us -> 65 us
    pallas_call x1, Pallas kernels: 67.1 us -> 65 us  [on_device(): pl.pallas_call(functools.partial(field_kernel, n_mode, n_space, blocks, t...]
where the time goes in v2:
time: 66.5 us; the launch traced here: 66.3 us
  Pallas kernels  65 us (98%)
  local copies, waits for them, and re-layouts  1.32 us (2%)
    pallas_call x1, Pallas kernels, on_device(): pl.pallas_call(functools.partial(field_kernel, n_mode, n_space, blocks, t...  65 us

profile of v2, /device:TPU:9, one launch (start us, length us, event | category | flops | bytes accessed | tf_op | source)
XLA Modules:
  0.0 66.3 jit_solution(16452291655117871502)
XLA Ops:
  0.0 65.0 %field.1 = bf16[4,256,1024]{2,1,0:T(8,128)(2,1)S(1)} custom-call(s32[4]{0:T(128)} %time_hbm.1, s32[4]{0:T(128)} %mom_hbm.1, s32[32]{0:T(128)} %bitcast.7, bf16[2,8192,256]{2,1,0:T(8,128)(2,1)} %bitcast.5, bf16[2,768,256]{2,1,0:T(8,128)(2,1)} %bitcast.6, bf16[4,384,1024]{2,1,0:T(8,128)(2,1)} %ins_hbm.1), custom_call_target="tpu_custom_call" | custom-call | tf_op jit(solution)/shard_map/field/pallas_call | solution.py:395
  65.0 1.3 %copy.8 = bf16[4,2,128,1024]{3,2,1,0:T(8,128)(2,1)} copy(bf16[4,2,128,1024]{3,2,1,0:T(8,128)(2,1)S(1)} %bitcast.4) | data formatting | bytes 4194304
